TPU v7x, 768 devices: a whole 4x8x12 slice. The times are simulated.
768 devices in a mesh: dp: 32 (over y_hi, x, core), ctx: 24 (over z, y_lo).
Axes of the slice: x: 4, y: 8 (y_hi: 4, y_lo: 2; y = y_hi * 2 + y_lo), z: 12, core: 2. Of those that a mesh axis runs over, the one named last changes fastest.
Arguments:
- queries: bfloat16 [110592, 2048], P(('dp', 'ctx')), parts along dimension 0, may hold values from -40 to 40
- keys: bfloat16 [110592, 2048], P(('dp', 'ctx')), parts along dimension 0, may hold values from -40 to 40
- values: bfloat16 [110592, 2048], P(('dp', 'ctx')), parts along dimension 0, may hold values from -6 to 6
- span_starts: int32 [192], P('dp'), parts along dimension 0, may hold values from 0 to 3168, as said below
Outputs:
- attended: bfloat16 [110592, 2048], P(('dp', 'ctx')), parts along dimension 0
There are 32 independent parts, one for each index of `dp`. A program takes and returns all parts, laid end to end along the dimension named above; each array names one. Nothing has to cross between parts.
Inputs may be any that keep to these rules, and one draw needn't show every extreme that they name: `span_starts`: starts rise, and the 6 spans of 288 positions lie inside the document without intersecting.
All inputs are finite; a program needn't handle non-finite values.
Results may differ from a plain program's by a relative error of at most 0.0045.
Values may be sent and summed in bfloat16 or wider, within the bound.
No kernel may reach another device: no remote copies, remote signals or barrier semaphores. Data moves between devices by JAX's collectives and lax.ppermute only.
A program may use at most 128 MiB of HBM per device.

v0:
```python
import jax
import jax.numpy as jnp
from jax import lax
from jax.sharding import PartitionSpec as P

HEADS = 16
HD = 128
SPAN = 288


def span_number(positions, span_starts):
    span_count = span_starts.shape[0]
    inside = (positions[:, None] >= span_starts[None, :]) & (
        positions[:, None] < span_starts[None, :] + SPAN
    )
    labels = jnp.arange(span_count, dtype=jnp.int32) + 1
    return jnp.sum(jnp.where(inside, labels[None, :], 0), axis=1)


def fold_block(operands):
    state_now, visible, group_query, key_heads, value_heads = operands
    row_max, row_sum, weighted = state_now
    scores = jnp.einsum(
        "qhd,khd->hqk", group_query, key_heads, preferred_element_type=jnp.float32
    ) * HD ** (-0.5)
    scores = jnp.where(visible[None], scores, -1e30)
    new_max = jnp.maximum(row_max, jnp.max(scores, axis=2))
    rescale = jnp.exp(row_max - new_max)
    weights = jnp.where(visible[None], jnp.exp(scores - new_max[:, :, None]), 0.0)
    new_sum = jnp.sum(weights, axis=2)
    products = jnp.einsum(
        "hqk,khd->qhd",
        weights.astype(jnp.bfloat16),
        value_heads,
        preferred_element_type=jnp.float32,
    )
    new_weighted = weighted * rescale.T[:, :, None] + products
    return (new_max, new_sum, new_weighted)


def keep_block(operands):
    return operands[0]


def body(queries, keys, values, span_starts):
    tok_rows = queries.shape[0]
    row_width = queries.shape[1]
    loop_index = lax.axis_index("ctx")
    local_rows = jnp.arange(tok_rows, dtype=jnp.int32)
    query_pos = loop_index * tok_rows + local_rows
    query_span = span_number(query_pos, span_starts)
    query_heads = queries.reshape(tok_rows, HEADS, HD)
    group_count = 2
    group_rows = tok_rows // group_count
    empty_state = tuple(
        (
            (
                jnp.full((HEADS, group_rows), -1e30, jnp.float32),
                jnp.zeros((HEADS, group_rows), jnp.float32),
                jnp.zeros((group_rows, HEADS, HD), jnp.float32),
            )
            for number in range(group_count)
        )
    )
    key_block = lax.all_gather(keys, "ctx", axis=0, tiled=True)
    value_block = lax.all_gather(values, "ctx", axis=0, tiled=True)
    block_rows = key_block.shape[0]
    key_pos = jnp.arange(block_rows, dtype=jnp.int32)
    key_span = span_number(key_pos, span_starts)
    key_heads = key_block.reshape(block_rows, HEADS, HD)
    value_heads = value_block.reshape(block_rows, HEADS, HD)
    updated = []
    for group_index in range(group_count):
        row_start = group_index * group_rows
        group_pos = query_pos[row_start : row_start + group_rows]
        group_span = query_span[row_start : row_start + group_rows]
        group_query = query_heads[row_start : row_start + group_rows]
        visible = (key_pos[None, :] <= group_pos[:, None]) | (
            group_span[:, None] == key_span[None, :]
        ) & (group_span[:, None] > 0)
        operands = (empty_state[group_index], visible, group_query, key_heads, value_heads)
        updated.append(lax.cond(jnp.any(visible), fold_block, keep_block, operands))
    final_state = tuple(updated)
    pieces = [weighted / row_sum.T[:, :, None] for row_max, row_sum, weighted in final_state]
    attended = jnp.concatenate(pieces, axis=0).reshape(tok_rows, row_width).astype(jnp.bfloat16)
    return attended


def solution(mesh):
    placed = (P(("dp", "ctx"), None), P(("dp", "ctx"), None), P(("dp", "ctx"), None), P("dp"))
    return jax.shard_map(
        body, mesh=mesh, in_specs=placed, out_specs=P(("dp", "ctx"), None), check_vma=False
    )
```

profile of v0, /device:TPU:1, one launch (start us, length us, event | category | flops | bytes accessed | tf_op | source)
XLA Modules:
  0.0 739.3 jit_solution(17823070025790757313)
XLA Ops:
  6.5 0.7 all-gather.3.cloned.1.call-update
  7.3 0.7 all-gather.5.cloned.1.call-update
  8.0 0.7 iota_add_fusion.1
  8.7 0.7 select_reduce_fusion.1
  9.4 0.8 select_reduce_fusion
  10.2 0.1 fusion.51
  10.3 0.1 broadcast_compare_fusion.1
  10.4 0.1 fusion.52
  10.4 1.3 fusion.47
  13.0 315.0 %all-gather.3.cloned.1.call-done = bf16[3456,2048]{1,0:T(8,128)(2,1)} async-done(((bf16[144,2048]{1,0:T(8,128)(2,1)}), bf16[3456,2048]{1,0:T(8,128)(2,1)}) %all-gather.3.cloned.1.call-update) | async-done | bytes 14155792 | tf_op jit(solution)/shard_map/all_gather | solution.py:65
  327.9 17.4 %copy.26 = bf16[3456,2048]{0,1:T(8,128)(2,1)} copy(bf16[3456,2048]{1,0:T(8,128)(2,1)} %all-gather.3.cloned.1.call-done) | data formatting | bytes 28311552 | tf_op jit(solution)/shard_map/all_gather | solution.py:65
  345.3 297.5 %all-gather.5.cloned.1.call-done = bf16[3456,2048]{1,0:T(8,128)(2,1)} async-done(((bf16[144,2048]{1,0:T(8,128)(2,1)}), bf16[3456,2048]{1,0:T(8,128)(2,1)}) %all-gather.5.cloned.1.call-update) | async-done | bytes 14155792 | tf_op jit(solution)/shard_map/all_gather | solution.py:66
  642.8 17.7 %copy.27 = bf16[3456,2048]{0,1:T(8,128)(2,1)} copy(bf16[3456,2048]{1,0:T(8,128)(2,1)} %all-gather.5.cloned.1.call-done) | data formatting | bytes 28311552 | tf_op jit(solution)/shard_map/all_gather | solution.py:66
  660.5 35.2 %conditional.3 = (f32[16,72]{1,0:T(8,128)S(1)}, f32[72,16,128]{2,0,1:T(8,128)S(1)}) conditional(s32[]{:T(128)} %convert_element_type.17, () %tuple.23, (pred[72,3456]{1,0:T(8,128)(4,1)S(1)}, bf16[144,2048]{1,0:T(8,128)(2,1)S(1)}, bf16[3456,16,128]{0,2,1:T(8,128)(2,1)}, bf16[3456,16,128]{0,2,1:T(8,128)(2,1)}) %tuple.55), branch_computations={%region_8.9_spmd, %region_9.12_spmd} | conditional | flops 2090337408 | bytes 77755408 | solution.py:82
  660.5 14.6 %fusion.22 = (f32[16,72]{1,0:T(8,128)S(1)}, f32[16,72,3456]{2,1,0:T(8,128)}) fusion(pred[72,3456]{1,0:T(8,128)(4,1)S(1)} %get-tuple-element.29, bf16[3456,16,128]{0,2,1:T(8,128)(2,1)} %get-tuple-element.63, bf16[144,2048]{1,0:T(8,128)(2,1)S(1)} %get-tuple-element.30), kind=kOutput, calls=%fused_computation.24 | convolution fusion | flops 1031158656 | bytes 30629376 | tf_op jit(solution)/shard_map/cond/branch_1_fun/qhd,khd->hqk/dot_general | solution.py:23
  675.2 12.4 %fusion.35 = f32[72,16,128]{2,0,1:T(8,128)S(1)} fusion(bf16[3456,16,128]{0,2,1:T(8,128)(2,1)} %get-tuple-element.64, f32[16,72,3456]{2,1,0:T(8,128)} %get-tuple-element.76, f32[16,72]{1,0:T(8,128)S(1)} %get-tuple-element.74, pred[72,3456]{1,0:T(8,128)(4,1)S(1)} %get-tuple-element.29, f32[72,16]{0,1:T(8,128)S(1)} %get-tuple-element.73), kind=kOutput, calls=%fused_computation.34 | convolution fusion | flops 1039269888 | bytes 30928896 | tf_op jit(solution)/shard_map/cond/branch_1_fun/hqk,khd->qhd/dot_general | solution.py:31
  687.6 8.2 %fusion.24 = f32[16,72]{1,0:T(8,128)S(1)} fusion(f32[16,72,3456]{2,1,0:T(8,128)} %get-tuple-element.76, f32[16,72]{1,0:T(8,128)S(1)} %get-tuple-element.74, pred[72,3456]{1,0:T(8,128)(4,1)S(1)} %get-tuple-element.29), kind=kLoop, calls=%fused_computation.26 | loop fusion | flops 19905408 | bytes 16183296 | tf_op jit(solution)/shard_map/cond/branch_1_fun/reduce_sum | solution.py:30
  695.7 0.2 divide_convert_fusion
  696.0 35.4 %conditional.2 = (f32[16,72]{1,0:T(8,128)S(1)}, f32[72,16,128]{2,0,1:T(8,128)S(1)}) conditional(s32[]{:T(128)} %convert_element_type.16, () %tuple.21, (pred[72,3456]{1,0:T(8,128)(4,1)S(1)}, bf16[144,2048]{1,0:T(8,128)(2,1)S(1)}, bf16[3456,16,128]{0,2,1:T(8,128)(2,1)}, bf16[3456,16,128]{0,2,1:T(8,128)(2,1)}) %tuple.56), branch_computations={%region_3.4_spmd, %region_4.7_spmd} | conditional | flops 2090337408 | bytes 77755408 | solution.py:82
  696.2 14.6 %fusion = (f32[16,72]{1,0:T(8,128)S(1)}, f32[16,72,3456]{2,1,0:T(8,128)}) fusion(pred[72,3456]{1,0:T(8,128)(4,1)S(1)} %get-tuple-element.25, bf16[3456,16,128]{0,2,1:T(8,128)(2,1)} %get-tuple-element.59, bf16[144,2048]{1,0:T(8,128)(2,1)S(1)} %get-tuple-element.26), kind=kOutput, calls=%fused_computation.2 | convolution fusion | flops 1031158656 | bytes 30629376 | tf_op jit(solution)/shard_map/cond/branch_1_fun/qhd,khd->hqk/dot_general | solution.py:23
  710.8 12.4 %fusion.13 = f32[72,16,128]{2,0,1:T(8,128)S(1)} fusion(bf16[3456,16,128]{0,2,1:T(8,128)(2,1)} %get-tuple-element.60, f32[16,72,3456]{2,1,0:T(8,128)} %get-tuple-element.72, f32[16,72]{1,0:T(8,128)S(1)} %get-tuple-element.70, pred[72,3456]{1,0:T(8,128)(4,1)S(1)} %get-tuple-element.25, f32[72,16]{0,1:T(8,128)S(1)} %get-tuple-element.69), kind=kOutput, calls=%fused_computation.12 | convolution fusion | flops 1039269888 | bytes 30928896 | tf_op jit(solution)/shard_map/cond/branch_1_fun/hqk,khd->qhd/dot_general | solution.py:31
  723.2 8.2 %fusion.2 = f32[16,72]{1,0:T(8,128)S(1)} fusion(f32[16,72,3456]{2,1,0:T(8,128)} %get-tuple-element.72, f32[16,72]{1,0:T(8,128)S(1)} %get-tuple-element.70, pred[72,3456]{1,0:T(8,128)(4,1)S(1)} %get-tuple-element.25), kind=kLoop, calls=%fused_computation.4 | loop fusion | flops 19905408 | bytes 16183296 | tf_op jit(solution)/shard_map/cond/branch_1_fun/reduce_sum | solution.py:30
  731.3 0.2 divide_convert_fusion.1
  731.6 0.9 copy_bitcast_fusion
  (7 shorter events, 0.1 us)
Async XLA Ops:
  6.5 321.4 %all-gather.3.cloned.1.call-start = ((), (), s32[]{:S(2)}) async-start(), calls=%async_computation | async-start | bytes 14745600 | tf_op jit(solution)/shard_map/all_gather | solution.py:65
  7.3 635.6 %all-gather.5.cloned.1.call-start = ((), (), s32[]{:S(2)}) async-start(), calls=%async_computation.1 | async-start | bytes 14745600 | tf_op jit(solution)/shard_map/all_gather | solution.py:66
  345.3 315.2 %copy-start = (bf16[144,2048]{1,0:T(8,128)(2,1)S(1)}, bf16[144,2048]{1,0:T(8,128)(2,1)}, u32[]{:S(2)}) copy-start(bf16[144,2048]{1,0:T(8,128)(2,1)} %param.8) | copy-start | bytes 1769476
Sparse Core Ops, SparseCore 0:
  9.7 318.1 all-gather.2
  330.3 312.4 all-gather.4
where the time goes:
time: 740 us; the launch traced here: 739 us
  waiting for transfers between devices  614 us (83%)
  matrix products  54 us (7%)
  local copies, waits for them, and re-layouts  35.3 us (5%)
  other arithmetic  21.2 us (3%)
  between operations  14.7 us (2%)
    all_gather x1, waiting for transfers between devices, body(): key_block = lax.all_gather(keys, 'ctx', axis=0, tiled=True)  315 us
    all_gather x1, waiting for transfers between devices, body(): value_block = lax.all_gather(values, 'ctx', axis=0, tiled=True)  298 us
    dot_general x2, matrix products, fold_block(): jnp.einsum('qhd,khd->hqk', group_query, key_heads, preferred_element_type...  29.2 us
    dot_general x2, matrix products, fold_block(): jnp.einsum('hqk,khd->qhd', weights.astype(jnp.bfloat16), value_heads, pre...  24.8 us
    all_gather x1, local copies, waits for them, and re-layouts, body(): value_block = lax.all_gather(values, 'ctx', axis=0, tiled=True)  17.7 us
    all_gather x1, local copies, waits for them, and re-layouts, body(): key_block = lax.all_gather(keys, 'ctx', axis=0, tiled=True)  17.4 us
    reduce_sum x2, other arithmetic, fold_block(): new_sum = jnp.sum(weights, axis=2)  16.3 us
  transfers between devices with their start and end apart: 2, of which 2 were waited for; matrix products, arithmetic and copies ran while one was open for 3% of the time, Pallas kernels for 0%

commit v1 on v0

v1 whole, which is shorter than its diff:
```python
import functools

import jax
import jax.numpy as jnp
from jax import lax
from jax.experimental import pallas as pl
from jax.experimental.pallas import tpu as pltpu
from jax.sharding import PartitionSpec as P

HEADS = 16
HD = 128
SPAN = 288
LOW = -1e30
GAIN = HD ** -0.5 * 1.4426950408889634

VMEM = pl.BlockSpec(memory_space=pltpu.VMEM)
SMEM = pl.BlockSpec(memory_space=pltpu.SMEM)


def head_of(slot):
    return slot // 3 * 2 + (slot % 3 == 2)


def pack_kernel(q_ref, k_ref, v_ref, out_ref):
    for slot in range(out_ref.shape[0]):
        cols = pl.ds(head_of(slot) * HD, HD)
        for part, ref in enumerate((q_ref, k_ref, v_ref)):
            out_ref[slot, :, part * HD : (part + 1) * HD] = ref[:, cols]


def unpack_kernel(in_ref, out_ref):
    for slot in range(in_ref.shape[0]):
        if slot % 3 != 1:
            out_ref[:, head_of(slot) * HD : (head_of(slot) + 1) * HD] = in_ref[slot]


def attend_kernel(starts_ref, qkv_ref, out_ref, acc_ref, top_ref, sum_ref, lim_ref, *, rows, keys, sub):
    length = qkv_ref.shape[0]
    spans = starts_ref.shape[0]
    groups = rows // sub
    lanes = 128
    columns = keys // lanes

    def query_block(block, carry):
        first = pl.multiple_of(block * rows, rows)
        last = first + rows - 1
        reach = last + 1
        pos = first + lax.broadcasted_iota(jnp.int32, (rows, lanes), 0)
        limit = pos + 1
        for i in range(spans):
            start = starts_ref[i]
            end = start + SPAN
            reach = jnp.where((start <= last) & (end > first), jnp.maximum(reach, end), reach)
            limit = jnp.where((pos >= start) & (pos < end), end, limit)
        lim_ref[...] = limit
        top_ref[...] = jnp.full_like(top_ref, LOW)
        sum_ref[...] = jnp.zeros_like(sum_ref)
        acc_ref[...] = jnp.zeros_like(acc_ref)

        def tile(number, masked):
            key0 = pl.multiple_of(number * keys, keys)
            key = qkv_ref[pl.ds(key0, keys), HD : 2 * HD]
            value = qkv_ref[pl.ds(key0, keys), 2 * HD :]

            def score(g):
                query = qkv_ref[pl.ds(first + g * sub, sub), :HD]
                return lax.dot_general(
                    query, key, (((1,), (1,)), ((), ())), preferred_element_type=jnp.float32
                )

            def weights(g, scores):
                at = pl.ds(g * sub, sub)
                parts = [scores[:, j * lanes : (j + 1) * lanes] for j in range(columns)]
                if masked:
                    room = lim_ref[at, :] - key0
                    lane = lax.broadcasted_iota(jnp.int32, (sub, lanes), 1)
                    parts = [jnp.where(lane + j * lanes < room, x, LOW) for j, x in enumerate(parts)]
                old = top_ref[at, :]
                top = functools.reduce(jnp.maximum, parts)
                new = jnp.maximum(old, jnp.max(top, axis=1, keepdims=True))
                fade = jnp.exp2((old - new) * GAIN)
                parts = [jnp.exp2((x - new) * GAIN) for x in parts]
                sum_ref[at, :] = sum_ref[at, :] * fade + functools.reduce(jnp.add, parts)
                top_ref[at, :] = new
                return fade, jnp.concatenate([x.astype(jnp.bfloat16) for x in parts], axis=1)

            def weigh(g, fade, low):
                at = pl.ds(g * sub, sub)
                product = jnp.dot(low, value, preferred_element_type=jnp.float32)
                acc_ref[at, :] = acc_ref[at, :] * fade + product

            scores = {g: score(g) for g in range(min(2, groups))}
            pending = None
            for g in range(groups):
                if g + 2 < groups:
                    scores[g + 2] = score(g + 2)
                current = (g, *weights(g, scores.pop(g)))
                if pending is not None:
                    weigh(*pending)
                pending = current
            weigh(*pending)

        def plain(number, carry):
            tile(number, False)
            return carry

        def masked(number, carry):
            tile(number, True)
            return carry

        full = (first + 1) // keys
        lax.fori_loop(0, full, plain, 0)
        lax.fori_loop(full, (reach + keys - 1) // keys, masked, 0)
        total = jnp.sum(sum_ref[...], axis=1, keepdims=True)
        out_ref[pl.ds(first, rows), :] = (acc_ref[...] / total).astype(out_ref.dtype)
        return carry

    lax.fori_loop(0, length // rows, query_block, 0)


def attend(starts, qkv, rows, keys, sub):
    length = qkv.shape[0]
    return pl.pallas_call(
        functools.partial(attend_kernel, rows=rows, keys=keys, sub=sub),
        out_shape=jax.ShapeDtypeStruct((length, HD), jnp.bfloat16),
        in_specs=[SMEM, VMEM],
        out_specs=VMEM,
        scratch_shapes=[
            pltpu.VMEM((rows, HD), jnp.float32),
            pltpu.VMEM((rows, 128), jnp.float32),
            pltpu.VMEM((rows, 128), jnp.float32),
            pltpu.VMEM((rows, 128), jnp.int32),
        ],
        cost_estimate=pl.CostEstimate(
            flops=2 * length * length * HD,
            bytes_accessed=4 * length * HD * 2,
            transcendentals=length * length // 2,
        ),
        name="attend",
    )(starts, qkv)


def body(queries, keys, values, span_starts):
    rows = queries.shape[0]
    width = queries.shape[1]
    devices = lax.axis_size("ctx")
    packed = pl.pallas_call(
        pack_kernel,
        out_shape=jax.ShapeDtypeStruct((devices, rows, 3 * HD), queries.dtype),
        in_specs=[VMEM] * 3,
        out_specs=VMEM,
        name="pack",
    )(queries, keys, values)
    gathered = lax.all_to_all(packed, "ctx", 0, 0)
    qkv = gathered.reshape(devices * rows, 3 * HD)
    attended = attend(span_starts, qkv, 1152, 1152, 128)
    returned = lax.all_to_all(attended.reshape(devices, rows, HD), "ctx", 0, 0)
    return pl.pallas_call(
        unpack_kernel,
        out_shape=jax.ShapeDtypeStruct((rows, width), queries.dtype),
        in_specs=[VMEM],
        out_specs=VMEM,
        name="unpack",
    )(returned)


def solution(mesh):
    placed = (P(("dp", "ctx"), None), P(("dp", "ctx"), None), P(("dp", "ctx"), None), P("dp"))
    return jax.shard_map(
        body, mesh=mesh, in_specs=placed, out_specs=P(("dp", "ctx"), None), check_vma=False
    )
```

time: 740 us -> 179 us (0.24)
  waiting for transfers between devices: 614 us -> 0 us
  blocking collectives: 0 us -> 148 us
  matrix products: 54 us -> 0 us
  local copies, waits for them, and re-layouts: 35.3 us -> 0 us
  Pallas kernels: 0 us -> 28.8 us
  other arithmetic: 21.2 us -> 0 us
  between operations: 14.7 us -> 0.01 us
    all_gather x2 -> x0, waiting for transfers between devices: 612 us -> none  [the longest x1 315 us: body(): key_block = lax.all_gather(keys, 'ctx', axis=0, tiled=True)]
    all_to_all x0 -> x2, blocking collectives: none -> 148 us  [the longest x1 107 us: body(): gathered = lax.all_to_all(packed, 'ctx', 0, 0)]
    dot_general x4 -> x0, matrix products: 54 us -> none  [the longest x2 29.2 us: fold_block(): jnp.einsum('qhd,khd->hqk', group_query, key_heads, preferred_element_type...]
    all_gather x2 -> x0, local copies, waits for them, and re-layouts: 35.1 us -> none  [the longest x1 17.7 us: body(): value_block = lax.all_gather(values, 'ctx', axis=0, tiled=True)]
    pallas_call x0 -> x3, Pallas kernels: none -> 28.8 us  [the longest x1 23.3 us: attend(): pl.pallas_call(functools.partial(attend_kernel, rows=rows, keys=keys, sub...]
    reduce_sum x4 -> x0, other arithmetic: 17.8 us -> none  [the longest x2 16.3 us: fold_block(): new_sum = jnp.sum(weights, axis=2)]
  transfers between devices with their start and end apart: 2 -> 0, of which waited for: 2 -> 0; matrix products, arithmetic and copies ran while one was open for 3% -> 0% of each run, Pallas kernels for 0% -> 0%
where the time goes in v1:
time: 179 us; the launch traced here: 176 us
  blocking collectives  148 us (83%)
  Pallas kernels  28.8 us (16%)
    all_to_all x1, blocking collectives, body(): gathered = lax.all_to_all(packed, 'ctx', 0, 0)  107 us
    all_to_all x1, blocking collectives, body(): returned = lax.all_to_all(attended.reshape(devices, rows, HD), 'ctx', 0, 0)  40.4 us
    pallas_call x1, Pallas kernels, attend(): pl.pallas_call(functools.partial(attend_kernel, rows=rows, keys=keys, sub...  23.3 us

profile of v1, /device:TPU:1, one launch (start us, length us, event | category | flops | bytes accessed | tf_op | source)
XLA Modules:
  0.0 176.3 jit_solution(2700648952012547871)
XLA Ops:
  0.0 3.4 %pack.1 = bf16[24,144,384]{2,1,0:T(8,128)(2,1)} custom-call(bf16[144,2048]{1,0:T(8,128)(2,1)} %q_ref.1, bf16[144,2048]{1,0:T(8,128)(2,1)} %k_ref.1, bf16[144,2048]{1,0:T(8,128)(2,1)} %v_ref.1), custom_call_target="tpu_custom_call" | custom-call | tf_op jit(solution)/shard_map/pack/pallas_call | solution.py:147
  3.4 107.2 %all_to_all.10 = bf16[24,144,384]{2,1,0:T(8,128)(2,1)} all-to-all(bf16[24,144,384]{2,1,0:T(8,128)(2,1)} %pack.1), channel_id=1, replica_groups=mesh['dp'=32,'ctx'=24] {'ctx'}, dimensions={0} | all-to-all | bytes 5308416 | tf_op jit(solution)/shard_map/all_to_all | solution.py:154
  110.5 23.3 %attend.1 = bf16[3456,128]{1,0:T(8,128)(2,1)} custom-call(s32[6]{0:T(128)} %starts_ref.1, bf16[3456,384]{1,0:T(8,128)(2,1)} %bitcast.2), custom_call_target="tpu_custom_call" | custom-call | flops 3057647616 | bytes 3538944 | tf_op jit(solution)/shard_map/attend/pallas_call | solution.py:123
  133.8 40.4 %all_to_all.11.in_ref = bf16[24,144,128]{2,1,0:T(8,128)(2,1)} all-to-all(bf16[24,144,128]{2,1,0:T(8,128)(2,1)} %bitcast.3), channel_id=1, replica_groups=mesh['dp'=32,'ctx'=24] {'ctx'}, dimensions={0} | all-to-all | bytes 1769472 | tf_op jit(solution)/shard_map/all_to_all | solution.py:157
  174.2 2.1 %unpack.1 = bf16[144,2048]{1,0:T(8,128)(2,1)} custom-call(bf16[24,144,128]{2,1,0:T(8,128)(2,1)} %all_to_all.11.in_ref), custom_call_target="tpu_custom_call" | custom-call | tf_op jit(solution)/shard_map/unpack/pallas_call | solution.py:158

commit v2 on v0

v2 whole, which is shorter than its diff:
```python
import functools

import jax
import jax.numpy as jnp
from jax import lax
from jax.experimental import pallas as pl
from jax.experimental.pallas import tpu as pltpu
from jax.sharding import PartitionSpec as P


HD = 128
SPAN = 288
LANES = 128
LOW = -1e30
SUB = 192
GAIN = HD ** -0.5 * 1.4426950408889634
OUTER_LOW, RELAY, OUTER_HIGH = 0, 1, 2

VMEM = pl.BlockSpec(memory_space=pltpu.VMEM)
ANY = pl.BlockSpec(memory_space=pl.ANY)
HBM = pl.BlockSpec(memory_space=pltpu.HBM)
SMEM = pl.BlockSpec(memory_space=pltpu.SMEM)


def parity():
    return lax.rem(lax.axis_index("dp"), 2)


def pack_kernel(q_ref, k_ref, v_ref, out_ref, sem):
    shift = parity()
    planes = out_ref.shape[0] // 2
    copies = []
    for plane in range(planes):
        for side in range(2):
            slot = 2 * lax.rem(plane + shift, planes) + side
            head = (plane // 3 * 2 + side) * 2
            low, high = pl.ds(head * HD, HD), pl.ds((head + 1) * HD, HD)
            if plane % 3 == RELAY:
                parts = (q_ref, low), (q_ref, high)
            elif plane % 3 == OUTER_LOW:
                parts = (k_ref, low), (v_ref, low)
            else:
                parts = (k_ref, high), (v_ref, high)
            for at, (ref, columns) in enumerate(parts):
                source = ref.at[:, columns]
                target = out_ref.at[slot, :, pl.ds(at * HD, HD)]
                copies.append(pltpu.make_async_copy(source, target, sem.at[len(copies)]))
    for copy in copies:
        copy.start()
    for copy in copies:
        copy.wait()


def unpack_kernel(in_ref, out_ref, sem):
    shift = parity()
    planes = in_ref.shape[0] // 2
    own = in_ref.shape[1]
    half = own // 2
    copies = []

    def move(source, target):
        copies.append(pltpu.make_async_copy(source, target, sem.at[len(copies)]))

    for plane in range(planes):
        for side in range(2):
            slot = 2 * lax.rem(plane + shift, planes) + side
            head = (plane // 3 * 2 + side) * 2
            low, high = pl.ds(head * HD, HD), pl.ds((head + 1) * HD, HD)
            if plane % 3 == OUTER_LOW:
                move(in_ref.at[slot], out_ref.at[pl.ds(0, own), low])
            elif plane % 3 == OUTER_HIGH:
                move(in_ref.at[slot], out_ref.at[pl.ds(0, own), high])
            else:
                move(in_ref.at[slot, pl.ds(0, half)], out_ref.at[pl.ds(own, half), low])
                move(in_ref.at[slot, pl.ds(half, half)], out_ref.at[pl.ds(own, half), high])
    for copy in copies:
        copy.start()
    for copy in copies:
        copy.wait()


def role():
    planes = lax.axis_size("ctx") // 2
    return lax.rem(lax.axis_index("ctx") // 2 + planes - parity(), 3)


def attend_kernel(starts_ref, low_ref, high_ref, kv_ref, out_ref, lim_ref, *, stride, offset, sub):
    length = kv_ref.shape[0]
    rows = low_ref.shape[0]
    sources = length // stride
    share = rows // sources
    here = role()
    is_high = here == OUTER_HIGH

    def position(source):
        return source * stride + offset + lax.broadcasted_iota(jnp.int32, (share, LANES), 0)

    def limits():
        for source in range(sources):
            lim_ref[pl.ds(source * share, share), :] = position(source) + 1
        for i in range(starts_ref.shape[0]):
            start = starts_ref[i]
            end = start + SPAN
            for step in range((SPAN + stride - 2) // stride + 1):
                source = jnp.minimum(start // stride + step, sources - 1)
                at = pl.ds(pl.multiple_of(source * share, 16), share)
                pos = position(source)
                lim_ref[at, :] = jnp.where((pos >= start) & (pos < end), end, lim_ref[at, :])

    def width(g):
        last = ((g + 1) * sub // share - 1) * stride + offset + share - 1
        return min(-(-(last + SPAN) // LANES) * LANES, length)

    def score(g):
        at = pl.ds(g * sub, sub)
        query = jnp.where(is_high, high_ref[at, :], low_ref[at, :])
        key = kv_ref[: width(g), :HD]
        return lax.dot_general(
            query, key, (((1,), (1,)), ((), ())), preferred_element_type=jnp.float32
        )

    def weights(g, scores):
        at = pl.ds(g * sub, sub)
        parts = [scores[:, j * LANES : (j + 1) * LANES] for j in range(width(g) // LANES)]
        clear = (g * sub // share * stride + offset + 1) // LANES
        room = lim_ref[at, :]
        lane = lax.broadcasted_iota(jnp.int32, (sub, LANES), 1)
        parts = [
            x if j < clear else jnp.where(lane + j * LANES < room, x, LOW)
            for j, x in enumerate(parts)
        ]
        top = jnp.max(functools.reduce(jnp.maximum, parts), axis=1, keepdims=True)
        parts = [jnp.exp2((x - top) * GAIN) for x in parts]
        total = jnp.sum(functools.reduce(jnp.add, parts), axis=1, keepdims=True)
        return total, jnp.concatenate([x.astype(jnp.bfloat16) for x in parts], axis=1)

    def weigh(g, total, low):
        product = jnp.dot(low, kv_ref[: width(g), HD:], preferred_element_type=jnp.float32)
        out_ref[pl.ds(g * sub, sub), :] = (product / total).astype(out_ref.dtype)

    @pl.when(here != RELAY)
    def _():
        limits()
        groups = rows // sub
        scores = score(0)
        pending = None
        for g in range(groups):
            ahead = score(g + 1) if g + 1 < groups else None
            current = (g, *weights(g, scores))
            scores = ahead
            if pending is not None:
                weigh(*pending)
            pending = current
        weigh(*pending)

    @pl.when(here == RELAY)
    def _():
        out_ref[...] = jnp.zeros_like(out_ref)


def attend(starts, low, high, kv, stride, offset):
    rows = low.shape[0]
    return pl.pallas_call(
        functools.partial(attend_kernel, stride=stride, offset=offset, sub=SUB),
        out_shape=jax.ShapeDtypeStruct((rows, HD), jnp.bfloat16),
        in_specs=[SMEM, VMEM, VMEM, VMEM],
        out_specs=VMEM,
        scratch_shapes=[pltpu.VMEM((rows, LANES), jnp.int32)],
        cost_estimate=pl.CostEstimate(
            flops=2 * rows * kv.shape[0] * HD,
            bytes_accessed=(2 * rows + 2 * kv.shape[0]) * HD * 2,
            transcendentals=rows * kv.shape[0] // 2,
        ),
        compiler_params=pltpu.CompilerParams(vmem_limit_bytes=40 << 20),
        name="attend",
    )(starts, low, high, kv)


def merge_kernel(own_ref, low_ref, high_ref, out_ref, sem):
    half = out_ref.shape[1] // 2

    @pl.when(role() == RELAY)
    def _():
        copies = [
            pltpu.make_async_copy(ref, out_ref.at[:, pl.ds(at * half, half)], sem.at[at])
            for at, ref in enumerate((low_ref, high_ref))
        ]
        for copy in copies:
            copy.start()
        for copy in copies:
            copy.wait()


def body(queries, keys, values, span_starts):
    rows = queries.shape[0]
    width = queries.shape[1]
    devices = lax.axis_size("ctx")
    docs = lax.axis_size("dp")
    planes = devices // 2
    own = rows // 3 * 2
    packed = pl.pallas_call(
        pack_kernel,
        out_shape=jax.ShapeDtypeStruct((devices, rows, 2 * HD), queries.dtype),
        in_specs=[HBM] * 3,
        out_specs=VMEM,
        scratch_shapes=[pltpu.SemaphoreType.DMA((2 * devices,))],
        compiler_params=pltpu.CompilerParams(vmem_limit_bytes=62 << 20),
        name="pack",
    )(queries, keys, values)
    gathered = lax.all_to_all(packed, "ctx", 0, 0)
    kv = gathered.reshape(devices * rows, 2 * HD)

    def relay(block, step, back=False):
        pairs = []
        for doc in range(docs):
            for plane in range(RELAY, planes, 3):
                for side in range(2):
                    middle = 2 * ((plane + doc % 2) % planes) + side
                    outer = 2 * ((plane + step + doc % 2) % planes) + side
                    pair = (doc * devices + middle, doc * devices + outer)
                    pairs.append(pair[::-1] if back else pair)
        return lax.ppermute(block, ("dp", "ctx"), pairs)

    def queries_of(start, stop):
        parts = [gathered[:, start:stop, at * HD : (at + 1) * HD] for at in range(2)]
        sent = [relay(part, step) for part, step in zip(parts, (-1, 1))]
        return [part.reshape(-1, HD) for part in sent]

    tail = queries_of(own, rows)
    head = queries_of(0, own)
    lent = attend(span_starts, *tail, kv, rows, own).reshape(devices, rows - own, HD)
    lent = [relay(lent, step, True) for step in (-1, 1)]
    kept = attend(span_starts, *head, kv, rows, 0).reshape(devices, own, HD)
    shared = pl.pallas_call(
        merge_kernel,
        out_shape=jax.ShapeDtypeStruct(kept.shape, kept.dtype),
        in_specs=[ANY] * 3,
        out_specs=ANY,
        input_output_aliases={0: 0},
        scratch_shapes=[pltpu.SemaphoreType.DMA((2,))],
        compiler_params=pltpu.CompilerParams(vmem_limit_bytes=8 << 20),
        name="merge",
    )(kept, *lent)
    returned = lax.all_to_all(shared, "ctx", 0, 0)
    return pl.pallas_call(
        unpack_kernel,
        out_shape=jax.ShapeDtypeStruct((rows, width), queries.dtype),
        in_specs=[VMEM],
        out_specs=ANY,
        scratch_shapes=[pltpu.SemaphoreType.DMA((2 * devices,))],
        compiler_params=pltpu.CompilerParams(vmem_limit_bytes=8 << 20),
        name="unpack",
    )(returned)


def solution(mesh):
    placed = (P(("dp", "ctx"), None), P(("dp", "ctx"), None), P(("dp", "ctx"), None), P("dp"))
    return jax.shard_map(
        body, mesh=mesh, in_specs=placed, out_specs=P(("dp", "ctx"), None), check_vma=False
    )
```

time: 740 us -> 146 us (0.20)
  the two profiles are of different devices: /device:TPU:1 before, /device:TPU:46 now
where the time goes in v2:
time: 146 us
  blocking collectives  111 us (76%)
  Pallas kernels  17.6 us (12%)
  waiting for transfers between devices  10.8 us (7%)
  starting transfers between devices  5.95 us (4%)
    all_to_all x1, blocking collectives, body(): gathered = lax.all_to_all(packed, 'ctx', 0, 0)  80.5 us
    all_to_all x1, blocking collectives, body(): returned = lax.all_to_all(shared, 'ctx', 0, 0)  30.3 us
    pallas_call x2, Pallas kernels, attend(): pl.pallas_call(functools.partial(attend_kernel, stride=stride, offset=off...  13.2 us
    ppermute x6, waiting for transfers between devices, relay(): return lax.ppermute(block, ('dp', 'ctx'), pairs)  10.8 us
    ppermute x6, starting transfers between devices, relay(): return lax.ppermute(block, ('dp', 'ctx'), pairs)  5.95 us
    pallas_call x1, Pallas kernels, body(): pl.pallas_call(pack_kernel, out_shape=jax.ShapeDtypeStruct((devices, rows...  3.13 us
  transfers between devices with their start and end apart: 6, of which 1 were waited for; matrix products, arithmetic and copies ran while one was open for 0% of the time, Pallas kernels for 9%

profile of v2, /device:TPU:46, one launch (start us, length us, event | category | flops | bytes accessed | tf_op | source)
XLA Modules:
  0.0 145.8 jit_solution(10639586795336488684)
XLA Ops:
  0.0 3.1 %pack.1 = bf16[24,144,256]{2,1,0:T(8,128)(2,1)} custom-call(bf16[144,2048]{1,0:T(8,128)(2,1)} %q_ref.1, bf16[144,2048]{1,0:T(8,128)(2,1)} %k_ref.1, bf16[144,2048]{1,0:T(8,128)(2,1)} %v_ref.1), custom_call_target="tpu_custom_call" | custom-call | tf_op jit(solution)/shard_map/pack/pallas_call | solution.py:201
  3.1 80.5 %all_to_all.10 = bf16[24,144,256]{2,1,0:T(8,128)(2,1)S(1)} all-to-all(bf16[24,144,256]{2,1,0:T(8,128)(2,1)} %pack.1), channel_id=1, replica_groups=mesh['dp'=32,'ctx'=24] {'ctx'}, dimensions={0} | all-to-all | bytes 3538944 | tf_op jit(solution)/shard_map/all_to_all | solution.py:210
  83.6 0.0 copy-start
  83.6 0.2 fusion.1
  83.8 1.3 collective-permute-start
  85.1 0.7 collective-permute-start.1
  85.8 0.1 fusion
  86.0 1.3 collective-permute-start.2
  87.2 0.7 collective-permute-start.3
  87.9 10.8 %collective-permute-done.2 = bf16[24,48,128]{2,1,0:T(8,128)(2,1)S(1)} collective-permute-done((bf16[24,48,128]{2,1,0:T(8,128)(2,1)S(1)}, bf16[24,48,128]{2,1,0:T(8,128)(2,1)S(1)}, u32[]{:S(2)}, u32[]{:S(2)}) %collective-permute-start.2) | collective-permute-done | bytes 294944 | tf_op jit(solution)/shard_map/ppermute | solution.py:222
  98.8 0.0 collective-permute-done.3
  98.8 0.0 copy-done
  98.8 4.8 %attend.3 = bf16[1152,128]{1,0:T(8,128)(2,1)S(1)} custom-call(s32[6]{0:T(128)S(1)} %copy-done, bf16[1152,128]{1,0:T(8,128)(2,1)S(1)} %bitcast.14, bf16[1152,128]{1,0:T(8,128)(2,1)S(1)} %bitcast.15, bf16[3456,256]{1,0:T(8,128)(2,1)S(1)} %bitcast.7), custom_call_target="tpu_custom_call" | custom-call | flops 1019215872 | bytes 2359296 | tf_op jit(solution)/shard_map/attend/pallas_call | solution.py:163
  103.6 1.3 collective-permute-start.4
  104.9 0.7 collective-permute-start.5
  105.6 0.0 collective-permute-done
  105.6 0.0 collective-permute-done.1
  105.7 8.4 %attend.2 = bf16[2304,128]{1,0:T(8,128)(2,1)S(1)} custom-call(s32[6]{0:T(128)S(1)} %copy-done, bf16[2304,128]{1,0:T(8,128)(2,1)S(1)} %bitcast.10, bf16[2304,128]{1,0:T(8,128)(2,1)S(1)} %bitcast.11, bf16[3456,256]{1,0:T(8,128)(2,1)S(1)} %bitcast.8), custom_call_target="tpu_custom_call" | custom-call | flops 2038431744 | bytes 2949120 | tf_op jit(solution)/shard_map/attend/pallas_call | solution.py:163
  114.1 0.0 collective-permute-done.4.low_ref
  114.1 0.0 collective-permute-done.5.high_ref
  114.1 0.1 merge.1
  114.1 30.3 %all_to_all.11.in_ref = bf16[24,96,128]{2,1,0:T(8,128)(2,1)S(1)} all-to-all(bf16[24,96,128]{2,1,0:T(8,128)(2,1)S(1)} %merge.1), channel_id=1, replica_groups=mesh['dp'=32,'ctx'=24] {'ctx'}, dimensions={0} | all-to-all | bytes 1179648 | tf_op jit(solution)/shard_map/all_to_all | solution.py:244
  144.4 1.2 unpack.1
Async XLA Ops:
  83.6 15.2 %copy-start = (s32[6]{0:T(128)S(1)}, s32[6]{0:T(128)}, u32[]{:S(2)}) copy-start(s32[6]{0:T(128)} %starts_ref.3) | copy-start | bytes 76
  83.8 21.8 %collective-permute-start = (bf16[24,96,128]{2,1,0:T(8,128)(2,1)S(1)}, bf16[24,96,128]{2,1,0:T(8,128)(2,1)S(1)}, u32[]{:S(2)}, u32[]{:S(2)}) collective-permute-start(bf16[24,96,128]{2,1,0:T(8,128)(2,1)S(1)} %get-tuple-element.8), channel_id=1, source_target_pairs={{2,0},{3,1},{8,6},{9,7},{14,12},{15,13},{20,18},{21,19},{28,26},{2... | collective-permute-start | bytes 1769480 | tf_op jit(solution)/shard_map/ppermute | solution.py:222
  85.1 20.5 %collective-permute-start.1 = (bf16[24,96,128]{2,1,0:T(8,128)(2,1)S(1)}, bf16[24,96,128]{2,1,0:T(8,128)(2,1)S(1)}, u32[]{:S(2)}, u32[]{:S(2)}) collective-permute-start(bf16[24,96,128]{2,1,0:T(8,128)(2,1)S(1)} %get-tuple-element.7), channel_id=1, source_target_pairs={{2,4},{3,5},{8,10},{9,11},{14,16},{15,17},{20,22},{21,23},{28,30},... | collective-permute-start | bytes 1769480 | tf_op jit(solution)/shard_map/ppermute | solution.py:222
  86.0 12.8 %collective-permute-start.2 = (bf16[24,48,128]{2,1,0:T(8,128)(2,1)S(1)}, bf16[24,48,128]{2,1,0:T(8,128)(2,1)S(1)}, u32[]{:S(2)}, u32[]{:S(2)}) collective-permute-start(bf16[24,48,128]{2,1,0:T(8,128)(2,1)S(1)} %get-tuple-element.6), channel_id=1, source_target_pairs={{2,0},{3,1},{8,6},{9,7},{14,12},{15,13},{20,18},{21,19},{28,26},{2... | collective-permute-start | bytes 884744 | tf_op jit(solution)/shard_map/ppermute | solution.py:222
  87.2 11.5 %collective-permute-start.3 = (bf16[24,48,128]{2,1,0:T(8,128)(2,1)S(1)}, bf16[24,48,128]{2,1,0:T(8,128)(2,1)S(1)}, u32[]{:S(2)}, u32[]{:S(2)}) collective-permute-start(bf16[24,48,128]{2,1,0:T(8,128)(2,1)S(1)} %get-tuple-element.5), channel_id=1, source_target_pairs={{2,4},{3,5},{8,10},{9,11},{14,16},{15,17},{20,22},{21,23},{28,30},... | collective-permute-start | bytes 884744 | tf_op jit(solution)/shard_map/ppermute | solution.py:222
  103.6 10.4 %collective-permute-start.4 = (bf16[24,48,128]{2,1,0:T(8,128)(2,1)S(1)}, bf16[24,48,128]{2,1,0:T(8,128)(2,1)S(1)}, u32[]{:S(2)}, u32[]{:S(2)}) collective-permute-start(bf16[24,48,128]{2,1,0:T(8,128)(2,1)S(1)} %bitcast.12), channel_id=1, source_target_pairs={{0,2},{1,3},{6,8},{7,9},{12,14},{13,15},{18,20},{19,21},{26,28},{2... | collective-permute-start | bytes 884744 | tf_op jit(solution)/shard_map/ppermute | solution.py:222
  104.9 9.1 %collective-permute-start.5 = (bf16[24,48,128]{2,1,0:T(8,128)(2,1)S(1)}, bf16[24,48,128]{2,1,0:T(8,128)(2,1)S(1)}, u32[]{:S(2)}, u32[]{:S(2)}) collective-permute-start(bf16[24,48,128]{2,1,0:T(8,128)(2,1)S(1)} %bitcast.13), channel_id=1, source_target_pairs={{4,2},{5,3},{10,8},{11,9},{16,14},{17,15},{22,20},{23,21},{30,28},... | collective-permute-start | bytes 884744 | tf_op jit(solution)/shard_map/ppermute | solution.py:222

commit v3 on v2

--- a/solution.py
+++ b/solution.py
@@ -84,7 +84,7 @@
     return lax.rem(lax.axis_index("ctx") // 2 + planes - parity(), 3)
 
 
-def attend_kernel(starts_ref, low_ref, high_ref, kv_ref, out_ref, lim_ref, *, stride, offset, sub):
+def attend_kernel(starts_ref, low_ref, high_ref, kv_ref, out_ref, lim_ref, wide_ref, *, stride, offset, sub):
     length = kv_ref.shape[0]
     rows = low_ref.shape[0]
     sources = length // stride
@@ -130,23 +130,24 @@
             for j, x in enumerate(parts)
         ]
         top = jnp.max(functools.reduce(jnp.maximum, parts), axis=1, keepdims=True)
-        parts = [jnp.exp2((x - top) * GAIN) for x in parts]
-        total = jnp.sum(functools.reduce(jnp.add, parts), axis=1, keepdims=True)
-        return total, jnp.concatenate([x.astype(jnp.bfloat16) for x in parts], axis=1)
-
-    def weigh(g, total, low):
-        product = jnp.dot(low, kv_ref[: width(g), HD:], preferred_element_type=jnp.float32)
-        out_ref[pl.ds(g * sub, sub), :] = (product / total).astype(out_ref.dtype)
+        low = [jnp.exp2((x - top) * GAIN).astype(jnp.bfloat16) for x in parts]
+        return jnp.concatenate(low, axis=1)
+
+    def weigh(g, low):
+        product = jnp.dot(low, wide_ref[: width(g), :], preferred_element_type=jnp.float32)
+        out_ref[pl.ds(g * sub, sub), :] = (product[:, :HD] / product[:, HD:]).astype(out_ref.dtype)
 
     @pl.when(here != RELAY)
     def _():
         limits()
+        wide_ref[:, :HD] = kv_ref[:, HD:]
+        wide_ref[:, HD:] = jnp.ones((length, HD), jnp.bfloat16)
         groups = rows // sub
         scores = score(0)
         pending = None
         for g in range(groups):
             ahead = score(g + 1) if g + 1 < groups else None
-            current = (g, *weights(g, scores))
+            current = (g, weights(g, scores))
             scores = ahead
             if pending is not None:
                 weigh(*pending)
@@ -165,7 +166,7 @@
         out_shape=jax.ShapeDtypeStruct((rows, HD), jnp.bfloat16),
         in_specs=[SMEM, VMEM, VMEM, VMEM],
         out_specs=VMEM,
-        scratch_shapes=[pltpu.VMEM((rows, LANES), jnp.int32)],
+        scratch_shapes=[pltpu.VMEM((rows, LANES), jnp.int32), pltpu.VMEM((kv.shape[0], 2 * HD), jnp.bfloat16)],
         cost_estimate=pl.CostEstimate(
             flops=2 * rows * kv.shape[0] * HD,
             bytes_accessed=(2 * rows + 2 * kv.shape[0]) * HD * 2,
@@ -204,9 +205,9 @@
         in_specs=[HBM] * 3,
         out_specs=VMEM,
         scratch_shapes=[pltpu.SemaphoreType.DMA((2 * devices,))],
-        compiler_params=pltpu.CompilerParams(vmem_limit_bytes=62 << 20),
+        compiler_params=pltpu.CompilerParams(vmem_limit_bytes=8 << 20),
         name="pack",
-    )(queries, keys, values)
+    )(*(pltpu.with_memory_space_constraint(x, pltpu.HBM) for x in (queries, keys, values)))
     gathered = lax.all_to_all(packed, "ctx", 0, 0)
     kv = gathered.reshape(devices * rows, 2 * HD)
 

time: 146 us -> 144 us (0.986)
  the two profiles are of different devices: /device:TPU:46 before, /device:TPU:56 now
where the time goes in v3:
time: 144 us; the launch traced here: 143 us
  blocking collectives  111 us (77%)
  Pallas kernels  15.5 us (11%)
  waiting for transfers between devices  10.8 us (8%)
  starting transfers between devices  5.95 us (4%)
    all_to_all x1, blocking collectives, body(): gathered = lax.all_to_all(packed, 'ctx', 0, 0)  80.3 us
    all_to_all x1, blocking collectives, body(): returned = lax.all_to_all(shared, 'ctx', 0, 0)  30.3 us
    pallas_call x2, Pallas kernels, attend(): pl.pallas_call(functools.partial(attend_kernel, stride=stride, offset=off...  12.4 us
    ppermute x6, waiting for transfers between devices, relay(): return lax.ppermute(block, ('dp', 'ctx'), pairs)  10.8 us
    ppermute x6, starting transfers between devices, relay(): return lax.ppermute(block, ('dp', 'ctx'), pairs)  5.95 us
  transfers between devices with their start and end apart: 6, of which 1 were waited for; matrix products, arithmetic and copies ran while one was open for 0% of the time, Pallas kernels for 9%

profile of v3, /device:TPU:56, one launch (start us, length us, event | category | flops | bytes accessed | tf_op | source)
XLA Modules:
  0.0 143.5 jit_solution(11455389131489363923)
XLA Ops:
  0.0 1.9 %pack.1 = bf16[24,144,256]{2,1,0:T(8,128)(2,1)S(1)} custom-call(bf16[144,2048]{1,0:T(8,128)(2,1)} %q_ref.1, bf16[144,2048]{1,0:T(8,128)(2,1)} %k_ref.1, bf16[144,2048]{1,0:T(8,128)(2,1)} %v_ref.1), custom_call_target="tpu_custom_call" | custom-call | tf_op jit(solution)/shard_map/pack/pallas_call | solution.py:202
  1.9 80.3 %all_to_all.10 = bf16[24,144,256]{2,1,0:T(8,128)(2,1)S(1)} all-to-all(bf16[24,144,256]{2,1,0:T(8,128)(2,1)S(1)} %pack.1), channel_id=1, replica_groups=mesh['dp'=32,'ctx'=24] {'ctx'}, dimensions={0} | all-to-all | bytes 3538944 | tf_op jit(solution)/shard_map/all_to_all | solution.py:211
  82.2 0.0 copy-start
  82.2 0.2 fusion.1
  82.4 1.3 collective-permute-start
  83.7 0.7 collective-permute-start.1
  84.4 0.1 fusion
  84.5 1.3 collective-permute-start.2
  85.8 0.7 collective-permute-start.3
  86.5 10.8 %collective-permute-done.2 = bf16[24,48,128]{2,1,0:T(8,128)(2,1)S(1)} collective-permute-done((bf16[24,48,128]{2,1,0:T(8,128)(2,1)S(1)}, bf16[24,48,128]{2,1,0:T(8,128)(2,1)S(1)}, u32[]{:S(2)}, u32[]{:S(2)}) %collective-permute-start.2) | collective-permute-done | bytes 294944 | tf_op jit(solution)/shard_map/ppermute | solution.py:223
  97.3 0.0 collective-permute-done.3
  97.3 0.0 copy-done
  97.3 4.6 %attend.3 = bf16[1152,128]{1,0:T(8,128)(2,1)S(1)} custom-call(s32[6]{0:T(128)S(1)} %copy-done, bf16[1152,128]{1,0:T(8,128)(2,1)S(1)} %bitcast.14, bf16[1152,128]{1,0:T(8,128)(2,1)S(1)} %bitcast.15, bf16[3456,256]{1,0:T(8,128)(2,1)S(1)} %bitcast.7), custom_call_target="tpu_custom_call" | custom-call | flops 1019215872 | bytes 2359296 | tf_op jit(solution)/shard_map/attend/pallas_call | solution.py:164
  101.9 1.3 collective-permute-start.4
  103.2 0.7 collective-permute-start.5
  103.9 0.0 collective-permute-done
  103.9 0.0 collective-permute-done.1
  103.9 7.8 %attend.2 = bf16[2304,128]{1,0:T(8,128)(2,1)S(1)} custom-call(s32[6]{0:T(128)S(1)} %copy-done, bf16[2304,128]{1,0:T(8,128)(2,1)S(1)} %bitcast.10, bf16[2304,128]{1,0:T(8,128)(2,1)S(1)} %bitcast.11, bf16[3456,256]{1,0:T(8,128)(2,1)S(1)} %bitcast.8), custom_call_target="tpu_custom_call" | custom-call | flops 2038431744 | bytes 2949120 | tf_op jit(solution)/shard_map/attend/pallas_call | solution.py:164
  111.7 0.0 collective-permute-done.4.low_ref
  111.7 0.0 collective-permute-done.5.high_ref
  111.7 0.1 merge.1
  111.8 30.3 %all_to_all.11.in_ref = bf16[24,96,128]{2,1,0:T(8,128)(2,1)S(1)} all-to-all(bf16[24,96,128]{2,1,0:T(8,128)(2,1)S(1)} %merge.1), channel_id=1, replica_groups=mesh['dp'=32,'ctx'=24] {'ctx'}, dimensions={0} | all-to-all | bytes 1179648 | tf_op jit(solution)/shard_map/all_to_all | solution.py:245
  142.1 1.2 unpack.1
Async XLA Ops:
  82.2 15.2 %copy-start = (s32[6]{0:T(128)S(1)}, s32[6]{0:T(128)}, u32[]{:S(2)}) copy-start(s32[6]{0:T(128)} %starts_ref.3) | copy-start | bytes 76
  82.4 21.5 %collective-permute-start = (bf16[24,96,128]{2,1,0:T(8,128)(2,1)S(1)}, bf16[24,96,128]{2,1,0:T(8,128)(2,1)S(1)}, u32[]{:S(2)}, u32[]{:S(2)}) collective-permute-start(bf16[24,96,128]{2,1,0:T(8,128)(2,1)S(1)} %get-tuple-element.8), channel_id=1, source_target_pairs={{2,0},{3,1},{8,6},{9,7},{14,12},{15,13},{20,18},{21,19},{28,26},{2... | collective-permute-start | bytes 1769480 | tf_op jit(solution)/shard_map/ppermute | solution.py:223
  83.7 20.2 %collective-permute-start.1 = (bf16[24,96,128]{2,1,0:T(8,128)(2,1)S(1)}, bf16[24,96,128]{2,1,0:T(8,128)(2,1)S(1)}, u32[]{:S(2)}, u32[]{:S(2)}) collective-permute-start(bf16[24,96,128]{2,1,0:T(8,128)(2,1)S(1)} %get-tuple-element.7), channel_id=1, source_target_pairs={{2,4},{3,5},{8,10},{9,11},{14,16},{15,17},{20,22},{21,23},{28,30},... | collective-permute-start | bytes 1769480 | tf_op jit(solution)/shard_map/ppermute | solution.py:223
  84.5 12.8 %collective-permute-start.2 = (bf16[24,48,128]{2,1,0:T(8,128)(2,1)S(1)}, bf16[24,48,128]{2,1,0:T(8,128)(2,1)S(1)}, u32[]{:S(2)}, u32[]{:S(2)}) collective-permute-start(bf16[24,48,128]{2,1,0:T(8,128)(2,1)S(1)} %get-tuple-element.6), channel_id=1, source_target_pairs={{2,0},{3,1},{8,6},{9,7},{14,12},{15,13},{20,18},{21,19},{28,26},{2... | collective-permute-start | bytes 884744 | tf_op jit(solution)/shard_map/ppermute | solution.py:223
  85.8 11.5 %collective-permute-start.3 = (bf16[24,48,128]{2,1,0:T(8,128)(2,1)S(1)}, bf16[24,48,128]{2,1,0:T(8,128)(2,1)S(1)}, u32[]{:S(2)}, u32[]{:S(2)}) collective-permute-start(bf16[24,48,128]{2,1,0:T(8,128)(2,1)S(1)} %get-tuple-element.5), channel_id=1, source_target_pairs={{2,4},{3,5},{8,10},{9,11},{14,16},{15,17},{20,22},{21,23},{28,30},... | collective-permute-start | bytes 884744 | tf_op jit(solution)/shard_map/ppermute | solution.py:223
  101.9 9.8 %collective-permute-start.4 = (bf16[24,48,128]{2,1,0:T(8,128)(2,1)S(1)}, bf16[24,48,128]{2,1,0:T(8,128)(2,1)S(1)}, u32[]{:S(2)}, u32[]{:S(2)}) collective-permute-start(bf16[24,48,128]{2,1,0:T(8,128)(2,1)S(1)} %bitcast.12), channel_id=1, source_target_pairs={{0,2},{1,3},{6,8},{7,9},{12,14},{13,15},{18,20},{19,21},{26,28},{2... | collective-permute-start | bytes 884744 | tf_op jit(solution)/shard_map/ppermute | solution.py:223
  103.2 8.5 %collective-permute-start.5 = (bf16[24,48,128]{2,1,0:T(8,128)(2,1)S(1)}, bf16[24,48,128]{2,1,0:T(8,128)(2,1)S(1)}, u32[]{:S(2)}, u32[]{:S(2)}) collective-permute-start(bf16[24,48,128]{2,1,0:T(8,128)(2,1)S(1)} %bitcast.13), channel_id=1, source_target_pairs={{4,2},{5,3},{10,8},{11,9},{16,14},{17,15},{22,20},{23,21},{30,28},... | collective-permute-start | bytes 884744 | tf_op jit(solution)/shard_map/ppermute | solution.py:223

commit v4 on v3

--- a/solution.py
+++ b/solution.py
@@ -84,18 +84,17 @@
     return lax.rem(lax.axis_index("ctx") // 2 + planes - parity(), 3)
 
 
-def attend_kernel(starts_ref, low_ref, high_ref, kv_ref, out_ref, lim_ref, wide_ref, *, stride, offset, sub):
+def prepare_kernel(starts_ref, kv_ref, wide_ref, *lim_refs, stride, offsets):
     length = kv_ref.shape[0]
-    rows = low_ref.shape[0]
     sources = length // stride
-    share = rows // sources
-    here = role()
-    is_high = here == OUTER_HIGH
-
-    def position(source):
-        return source * stride + offset + lax.broadcasted_iota(jnp.int32, (share, LANES), 0)
-
-    def limits():
+    wide_ref[:, :HD] = kv_ref[:, HD:]
+    wide_ref[:, HD:] = jnp.ones((length, HD), jnp.bfloat16)
+    for offset, lim_ref in zip(offsets, lim_refs):
+        share = lim_ref.shape[0] // sources
+
+        def position(source):
+            return source * stride + offset + lax.broadcasted_iota(jnp.int32, (share, LANES), 0)
+
         for source in range(sources):
             lim_ref[pl.ds(source * share, share), :] = position(source) + 1
         for i in range(starts_ref.shape[0]):
@@ -106,6 +105,15 @@
                 at = pl.ds(pl.multiple_of(source * share, 16), share)
                 pos = position(source)
                 lim_ref[at, :] = jnp.where((pos >= start) & (pos < end), end, lim_ref[at, :])
+
+
+def attend_kernel(lim_ref, low_ref, high_ref, kv_ref, wide_ref, out_ref, *, stride, offset, sub):
+    length = kv_ref.shape[0]
+    rows = low_ref.shape[0]
+    sources = length // stride
+    share = rows // sources
+    here = role()
+    is_high = here == OUTER_HIGH
 
     def width(g):
         last = ((g + 1) * sub // share - 1) * stride + offset + share - 1
@@ -139,9 +147,6 @@
 
     @pl.when(here != RELAY)
     def _():
-        limits()
-        wide_ref[:, :HD] = kv_ref[:, HD:]
-        wide_ref[:, HD:] = jnp.ones((length, HD), jnp.bfloat16)
         groups = rows // sub
         scores = score(0)
         pending = None
@@ -159,14 +164,13 @@
         out_ref[...] = jnp.zeros_like(out_ref)
 
 
-def attend(starts, low, high, kv, stride, offset):
+def attend(limits, low, high, kv, wide, stride, offset):
     rows = low.shape[0]
     return pl.pallas_call(
         functools.partial(attend_kernel, stride=stride, offset=offset, sub=SUB),
         out_shape=jax.ShapeDtypeStruct((rows, HD), jnp.bfloat16),
-        in_specs=[SMEM, VMEM, VMEM, VMEM],
+        in_specs=[VMEM] * 5,
         out_specs=VMEM,
-        scratch_shapes=[pltpu.VMEM((rows, LANES), jnp.int32), pltpu.VMEM((kv.shape[0], 2 * HD), jnp.bfloat16)],
         cost_estimate=pl.CostEstimate(
             flops=2 * rows * kv.shape[0] * HD,
             bytes_accessed=(2 * rows + 2 * kv.shape[0]) * HD * 2,
@@ -174,7 +178,7 @@
         ),
         compiler_params=pltpu.CompilerParams(vmem_limit_bytes=40 << 20),
         name="attend",
-    )(starts, low, high, kv)
+    )(limits, low, high, kv, wide)
 
 
 def merge_kernel(own_ref, low_ref, high_ref, out_ref, sem):
@@ -229,9 +233,21 @@
 
     tail = queries_of(own, rows)
     head = queries_of(0, own)
-    lent = attend(span_starts, *tail, kv, rows, own).reshape(devices, rows - own, HD)
+    wide, tail_limits, head_limits = pl.pallas_call(
+        functools.partial(prepare_kernel, stride=rows, offsets=(own, 0)),
+        out_shape=(
+            jax.ShapeDtypeStruct(kv.shape, kv.dtype),
+            jax.ShapeDtypeStruct((devices * (rows - own), LANES), jnp.int32),
+            jax.ShapeDtypeStruct((devices * own, LANES), jnp.int32),
+        ),
+        in_specs=[SMEM, VMEM],
+        out_specs=(VMEM,) * 3,
+        compiler_params=pltpu.CompilerParams(vmem_limit_bytes=8 << 20),
+        name="prepare",
+    )(span_starts, kv)
+    lent = attend(tail_limits, *tail, kv, wide, rows, own).reshape(devices, rows - own, HD)
     lent = [relay(lent, step, True) for step in (-1, 1)]
-    kept = attend(span_starts, *head, kv, rows, 0).reshape(devices, own, HD)
+    kept = attend(head_limits, *head, kv, wide, rows, 0).reshape(devices, own, HD)
     shared = pl.pallas_call(
         merge_kernel,
         out_shape=jax.ShapeDtypeStruct(kept.shape, kept.dtype),

time: 144 us -> 142 us (0.986)
  the two profiles are of different devices: /device:TPU:56 before, /device:TPU:40 now
where the time goes in v4:
time: 142 us; the launch traced here: 141 us
  blocking collectives  111 us (78%)
  Pallas kernels  14.6 us (10%)
  waiting for transfers between devices  9.61 us (7%)
  starting transfers between devices  5.95 us (4%)
    all_to_all x1, blocking collectives, body(): gathered = lax.all_to_all(packed, 'ctx', 0, 0)  80.3 us
    all_to_all x1, blocking collectives, body(): returned = lax.all_to_all(shared, 'ctx', 0, 0)  30.4 us
    pallas_call x2, Pallas kernels, attend(): pl.pallas_call(functools.partial(attend_kernel, stride=stride, offset=off...  10.3 us
    ppermute x6, waiting for transfers between devices, relay(): return lax.ppermute(block, ('dp', 'ctx'), pairs)  9.61 us
    ppermute x6, starting transfers between devices, relay(): return lax.ppermute(block, ('dp', 'ctx'), pairs)  5.95 us
  transfers between devices with their start and end apart: 6, of which 1 were waited for; matrix products, arithmetic and copies ran while one was open for 0% of the time, Pallas kernels for 8%

profile of v4, /device:TPU:40, one launch (start us, length us, event | category | flops | bytes accessed | tf_op | source)
XLA Modules:
  0.0 141.5 jit_solution(3669907281044795477)
XLA Ops:
  0.0 1.9 %pack.1 = bf16[24,144,256]{2,1,0:T(8,128)(2,1)S(1)} custom-call(bf16[144,2048]{1,0:T(8,128)(2,1)} %q_ref.1, bf16[144,2048]{1,0:T(8,128)(2,1)} %k_ref.1, bf16[144,2048]{1,0:T(8,128)(2,1)} %v_ref.1), custom_call_target="tpu_custom_call" | custom-call | tf_op jit(solution)/shard_map/pack/pallas_call | solution.py:206
  1.9 80.3 %all_to_all.10 = bf16[24,144,256]{2,1,0:T(8,128)(2,1)S(1)} all-to-all(bf16[24,144,256]{2,1,0:T(8,128)(2,1)S(1)} %pack.1), channel_id=1, replica_groups=mesh['dp'=32,'ctx'=24] {'ctx'}, dimensions={0} | all-to-all | bytes 3538944 | tf_op jit(solution)/shard_map/all_to_all | solution.py:215
  82.2 0.0 copy-start
  82.2 0.2 fusion.1
  82.4 1.3 collective-permute-start
  83.7 0.7 collective-permute-start.1
  84.4 0.1 fusion
  84.5 1.3 collective-permute-start.2
  85.8 0.7 collective-permute-start.3
  86.5 0.0 copy-done
  86.5 1.2 prepare.1
  87.7 9.6 %collective-permute-done.2 = bf16[24,48,128]{2,1,0:T(8,128)(2,1)S(1)} collective-permute-done((bf16[24,48,128]{2,1,0:T(8,128)(2,1)S(1)}, bf16[24,48,128]{2,1,0:T(8,128)(2,1)S(1)}, u32[]{:S(2)}, u32[]{:S(2)}) %collective-permute-start.2) | collective-permute-done | bytes 294944 | tf_op jit(solution)/shard_map/ppermute | solution.py:227
  97.3 0.0 collective-permute-done.3
  97.3 3.6 %attend.3 = bf16[1152,128]{1,0:T(8,128)(2,1)S(1)} custom-call(s32[1152,128]{1,0:T(8,128)S(1)} %get-tuple-element.10.lim_ref, bf16[1152,128]{1,0:T(8,128)(2,1)S(1)} %bitcast.13, bf16[1152,128]{1,0:T(8,128)(2,1)S(1)} %bitcast.14, bf16[3456,256]{1,0:T(8,128)(2,1)S(1)} %bitcast.8, bf16[3456,256]{1,0:T(8,128)(2,1)S(1)} %get-tuple-element.9.wide_ref), custom_call_target="tpu_custom_call" | custom-call | flops 1019215872 | bytes 2359296 | tf_op jit(solution)/shard_map/attend/pallas_call | solution.py:169
  100.9 1.3 collective-permute-start.4
  102.2 0.7 collective-permute-start.5
  102.9 0.0 collective-permute-done
  102.9 0.0 collective-permute-done.1
  102.9 6.7 %attend.2 = bf16[2304,128]{1,0:T(8,128)(2,1)S(1)} custom-call(s32[2304,128]{1,0:T(8,128)S(1)} %get-tuple-element.8.lim_ref, bf16[2304,128]{1,0:T(8,128)(2,1)S(1)} %bitcast.15, bf16[2304,128]{1,0:T(8,128)(2,1)S(1)} %bitcast.16, bf16[3456,256]{1,0:T(8,128)(2,1)S(1)} %bitcast.9, bf16[3456,256]{1,0:T(8,128)(2,1)S(1)} %get-tuple-element.9.wide_ref), custom_call_target="tpu_custom_call" | custom-call | flops 2038431744 | bytes 2949120 | tf_op jit(solution)/shard_map/attend/pallas_call | solution.py:169
  109.6 0.0 collective-permute-done.4.low_ref
  109.6 0.0 collective-permute-done.5.high_ref
  109.7 0.1 merge.1
  109.7 30.4 %all_to_all.11.in_ref = bf16[24,96,128]{2,1,0:T(8,128)(2,1)S(1)} all-to-all(bf16[24,96,128]{2,1,0:T(8,128)(2,1)S(1)} %merge.1), channel_id=1, replica_groups=mesh['dp'=32,'ctx'=24] {'ctx'}, dimensions={0} | all-to-all | bytes 1179648 | tf_op jit(solution)/shard_map/all_to_all | solution.py:261
  140.1 1.2 unpack.1
Async XLA Ops:
  82.2 4.3 %copy-start = (s32[6]{0:T(128)S(1)}, s32[6]{0:T(128)}, u32[]{:S(2)}) copy-start(s32[6]{0:T(128)} %starts_ref.1) | copy-start | bytes 76
  82.4 20.5 %collective-permute-start = (bf16[24,96,128]{2,1,0:T(8,128)(2,1)S(1)}, bf16[24,96,128]{2,1,0:T(8,128)(2,1)S(1)}, u32[]{:S(2)}, u32[]{:S(2)}) collective-permute-start(bf16[24,96,128]{2,1,0:T(8,128)(2,1)S(1)} %get-tuple-element.14), channel_id=1, source_target_pairs={{2,0},{3,1},{8,6},{9,7},{14,12},{15,13},{20,18},{21,19},{28,26},{2... | collective-permute-start | bytes 1769480 | tf_op jit(solution)/shard_map/ppermute | solution.py:227
  83.7 19.2 %collective-permute-start.1 = (bf16[24,96,128]{2,1,0:T(8,128)(2,1)S(1)}, bf16[24,96,128]{2,1,0:T(8,128)(2,1)S(1)}, u32[]{:S(2)}, u32[]{:S(2)}) collective-permute-start(bf16[24,96,128]{2,1,0:T(8,128)(2,1)S(1)} %get-tuple-element.13), channel_id=1, source_target_pairs={{2,4},{3,5},{8,10},{9,11},{14,16},{15,17},{20,22},{21,23},{28,30},... | collective-permute-start | bytes 1769480 | tf_op jit(solution)/shard_map/ppermute | solution.py:227
  84.5 12.8 %collective-permute-start.2 = (bf16[24,48,128]{2,1,0:T(8,128)(2,1)S(1)}, bf16[24,48,128]{2,1,0:T(8,128)(2,1)S(1)}, u32[]{:S(2)}, u32[]{:S(2)}) collective-permute-start(bf16[24,48,128]{2,1,0:T(8,128)(2,1)S(1)} %get-tuple-element.12), channel_id=1, source_target_pairs={{2,0},{3,1},{8,6},{9,7},{14,12},{15,13},{20,18},{21,19},{28,26},{2... | collective-permute-start | bytes 884744 | tf_op jit(solution)/shard_map/ppermute | solution.py:227
  85.8 11.5 %collective-permute-start.3 = (bf16[24,48,128]{2,1,0:T(8,128)(2,1)S(1)}, bf16[24,48,128]{2,1,0:T(8,128)(2,1)S(1)}, u32[]{:S(2)}, u32[]{:S(2)}) collective-permute-start(bf16[24,48,128]{2,1,0:T(8,128)(2,1)S(1)} %get-tuple-element.11), channel_id=1, source_target_pairs={{2,4},{3,5},{8,10},{9,11},{14,16},{15,17},{20,22},{21,23},{28,30},... | collective-permute-start | bytes 884744 | tf_op jit(solution)/shard_map/ppermute | solution.py:227
  100.9 8.7 %collective-permute-start.4 = (bf16[24,48,128]{2,1,0:T(8,128)(2,1)S(1)}, bf16[24,48,128]{2,1,0:T(8,128)(2,1)S(1)}, u32[]{:S(2)}, u32[]{:S(2)}) collective-permute-start(bf16[24,48,128]{2,1,0:T(8,128)(2,1)S(1)} %bitcast.11), channel_id=1, source_target_pairs={{0,2},{1,3},{6,8},{7,9},{12,14},{13,15},{18,20},{19,21},{26,28},{2... | collective-permute-start | bytes 884744 | tf_op jit(solution)/shard_map/ppermute | solution.py:227
  102.2 7.4 %collective-permute-start.5 = (bf16[24,48,128]{2,1,0:T(8,128)(2,1)S(1)}, bf16[24,48,128]{2,1,0:T(8,128)(2,1)S(1)}, u32[]{:S(2)}, u32[]{:S(2)}) collective-permute-start(bf16[24,48,128]{2,1,0:T(8,128)(2,1)S(1)} %bitcast.12), channel_id=1, source_target_pairs={{4,2},{5,3},{10,8},{11,9},{16,14},{17,15},{22,20},{23,21},{30,28},... | collective-permute-start | bytes 884744 | tf_op jit(solution)/shard_map/ppermute | solution.py:227
